TPU v7x, 128 devices: a whole 4x4x4 slice. The times are simulated.
128 devices in a mesh: space: 8 (over x, z_lo), filt: 16 (over z_hi, y, core).
Axes of the slice: x: 4, y: 4, z: 4 (z_hi: 2, z_lo: 2; z = z_hi * 2 + z_lo), core: 2. Of those that a mesh axis runs over, the one named last changes fastest.
Arguments:
- layer_input: bfloat16 [32, 64, 32, 128], P('space', 'filt'), may hold values from -6 to 6
- first_kernel: bfloat16 [256, 3456], replicated, may hold values from -0.109375 to 0.109375
- second_kernel: bfloat16 [512, 6912], replicated, may hold values from -0.078125 to 0.078125
- cotangent: bfloat16 [512, 16, 512], P('filt', 'space'), may hold values from -0.29882812 to 0.29882812
Outputs:
- activation: float32 [512, 16, 512], P('filt', 'space')
- kernel_grad: float32 [256, 3456], P(('space', 'filt'))
All inputs are finite; a program needn't handle non-finite values.
Results may differ from a plain program's by a relative error of at most 0.0055.
Values may be sent and summed in bfloat16 or wider, within the bound.
No kernel may reach another device: no remote copies, remote signals or barrier semaphores. Data moves between devices by JAX's collectives and lax.ppermute only.
A program may use at most 64 MiB of HBM per device.

v0:
```python
import jax
import jax.numpy as jnp
from jax import lax
from jax.experimental import pallas as pl
from jax.experimental.pallas import tpu as pltpu
from jax.sharding import PartitionSpec as P


BOTH = ("space", "filt")
F32 = jnp.float32
BF16 = jnp.bfloat16
VMEM = pl.BlockSpec(memory_space=pltpu.VMEM)
HBM = pl.BlockSpec(memory_space=pltpu.HBM)


def nt(left, right):
    return lax.dot_general(left, right, (((1,), (1,)), ((), ())), preferred_element_type=F32)


def nn(left, right):
    return lax.dot_general(left, right, (((1,), (0,)), ((), ())), preferred_element_type=F32)


def sigmoid(v):
    return 1.0 / (1.0 + jnp.exp(-v))


def shifted(v, step):
    rows = v.shape[1]
    wide = v.astype(F32)
    at = lax.broadcasted_iota(jnp.int32, wide.shape, 1)
    moved = pltpu.roll(wide, (-step) % rows, 1)
    edge = rows - 1 if step > 0 else 0
    return jnp.where(at == edge, 0.0, moved).astype(BF16)


def first_kernel_body(own, xm, xp, off, pair, w1, xc_out, slope_out, pooled_out, xc):
    space_at = lax.axis_index("space")
    filt_at = lax.axis_index("filt")
    parity = lax.rem(filt_at, 2)
    off_y = parity * 7
    pair_y = 7 - parity * 7

    def put(piece, x0, y0):
        nx, ny = piece.shape[:2]
        v = piece[...].reshape(nx * ny, 16, 256)
        even, odd = v[:, :, :128], v[:, :, 128:]
        where = (pl.ds(x0, nx), pl.ds(y0, ny))
        shape = (nx, ny, 16, 128)
        xc[where + (slice(None), slice(0, 128))] = shifted(odd, -1).reshape(shape)
        xc[where + (slice(None), slice(128, 256))] = even.reshape(shape)
        xc[where + (slice(None), slice(256, 384))] = odd.reshape(shape)
        xc[where + (slice(None), slice(384, 512))] = shifted(even, 1).reshape(shape)

    put(own, 3, 3)
    put(xm, 0, 3)
    put(xp, 7, 3)
    put(off, 0, off_y)
    put(pair, 0, pair_y)
    xc_out[...] = xc[2:8, 2:8]

    for plane in range(4):
        total = None
        for r in range(2):
            pre = None
            for a in range(3):
                lhs = jnp.concatenate(
                    [
                        xc[2 * plane + a : 2 * plane + a + 2, b : b + 8, :, r * 128 : r * 128 + 384].reshape(256, 384)
                        for b in range(3)
                    ],
                    axis=1,
                )
                part = nt(lhs, w1[:, a * 1152 : (a + 1) * 1152])
                pre = part if pre is None else pre + part
            pre = pre.reshape(2, 8, 16, 256)
            logistic = sigmoid(pre)
            if plane in (1, 2):
                inner, gate = pre[:, 2:6], logistic[:, 2:6]
                slope_out[r, 2 * plane - 2 : 2 * plane] = gate * (1.0 + inner * (1.0 - gate))
            value = (pre * logistic).reshape(2, 4, 2, 16, 256)
            value = (value[0, :, 0] + value[0, :, 1]) + (value[1, :, 0] + value[1, :, 1])
            total = value if total is None else total + value
        row = lax.broadcasted_iota(jnp.int32, total.shape, 0)
        keep = ((row > 0) | (filt_at > 0)) & ((row < 3) | (filt_at < 15))
        if plane == 0:
            keep = keep & (space_at > 0)
        if plane == 3:
            keep = keep & (space_at < 7)
        pooled_out[plane] = jnp.where(keep, total * 0.125, 0.0).astype(BF16)


def load_chunks(w2_hbm, w2, sem):
    loads = []
    for t in range(9):
        lanes = slice(t * 768, (t + 1) * 768)
        loads.append(pltpu.make_async_copy(w2_hbm.at[:, lanes], w2.at[:, lanes], sem.at[t]))
        loads[-1].start()
    return loads


def second_kernel_body(pooled, cot, w2_hbm, act_out, g2_out, pc, w2, sem):
    loads = load_chunks(w2_hbm, w2, sem)
    v = pooled[...].reshape(16, 16, 256)
    pc[:, :, :, 0:256] = shifted(v, -1).reshape(4, 4, 16, 256)
    pc[:, :, :, 256:512] = pooled[...]
    pc[:, :, :, 512:768] = shifted(v, 1).reshape(4, 4, 16, 256)
    pre = None
    for a in range(3):
        for b in range(3):
            t = 3 * a + b
            loads[t].wait()
            cells = pc[a : a + 2, b : b + 2].reshape(64, 768)
            part = nt(w2[:, t * 768 : (t + 1) * 768], cells)
            pre = part if pre is None else pre + part
    logistic = sigmoid(pre)
    act_out[...] = (pre * logistic).astype(act_out.dtype)
    grad = cot[...].astype(F32) * (logistic * (1.0 + pre * (1.0 - logistic)))
    g2_out[...] = jnp.transpose(grad).astype(BF16).reshape(2, 2, 16, 512)


def backward_kernel(own, xm, xp, off, pair, slope, xc, w2_hbm, keep_out, send_out, gc, w2, sem):
    loads = load_chunks(w2_hbm, w2, sem)
    parity = lax.rem(lax.axis_index("filt"), 2)
    off_y = parity * 3
    pair_y = 3 - parity * 3

    def put(piece, x0, y0):
        nx, ny = piece.shape[:2]
        v = piece[...].reshape(nx * ny, 16, 512)
        where = (pl.ds(x0, nx), pl.ds(y0, ny))
        shape = (nx, ny, 16, 512)
        gc[where + (slice(None), slice(0, 512))] = shifted(v, 1).reshape(shape)
        gc[where + (slice(None), slice(512, 1024))] = v.reshape(shape)
        gc[where + (slice(None), slice(1024, 1536))] = shifted(v, -1).reshape(shape)

    put(own, 1, 1)
    put(xm, 0, 1)
    put(xp, 3, 1)
    put(off, 0, off_y)
    put(pair, 0, pair_y)

    acc = None
    for a in range(3):
        for b in range(3):
            t = 3 * a + b
            loads[t].wait()
            for c in range(3):
                cells = gc[2 - a : 4 - a, 2 - b : 4 - b, :, c * 512 : (c + 1) * 512].reshape(64, 512)
                part = nn(cells, w2[:, (3 * t + c) * 256 : (3 * t + c + 1) * 256])
                acc = part if acc is None else acc + part
    acc = (acc * 0.125).reshape(2, 2, 16, 256)

    row = lax.broadcasted_iota(jnp.int32, (256, 256), 0)
    column = lax.broadcasted_iota(jnp.int32, (256, 256), 1)
    half = row // 128
    inside = row - half * 128
    want = 4 * (inside // 2) + lax.rem(inside, 2) + 2 * jnp.where(half == 0, parity, 1 - parity)
    order = jnp.where(column == want, 1.0, 0.0).astype(BF16)
    turned = []
    for r in range(2):
        grads = [
            (acc[x // 2, y // 2] * slope[r, x, y]).astype(BF16)
            for x in range(4)
            for y in range(4)
        ]
        turned.append(nt(order, jnp.concatenate(grads, axis=0)).astype(BF16))
    for a in range(3):
        for b in range(3):
            t = 3 * a + b
            part = None
            for r in range(2):
                cells = xc[a : a + 4, b : b + 4, :, r * 128 : r * 128 + 384].reshape(256, 384)
                one = nn(turned[r], cells)
                part = one if part is None else part + one
            part = part.astype(BF16)
            keep_out[:, t * 384 : (t + 1) * 384] = part[:128]
            send_out[:, t * 384 : (t + 1) * 384] = part[128:]


def route(step, across, spaces, filts):
    pairs = []
    for i in range(spaces):
        for j in range(filts):
            to_i = i + step
            to_j = (j + 1 if j % 2 else j - 1) if across else j
            if 0 <= to_i < spaces and 0 <= to_j < filts:
                pairs.append((i * filts + j, to_i * filts + to_j))
    return pairs


def surround(x, width):
    spaces, filts = lax.axis_size("space"), lax.axis_size("filt")
    length = x.shape[1]
    parity = lax.rem(lax.axis_index("filt"), 2)
    far = parity * (length - width)
    near = (length - width) - far
    last, first = x[x.shape[0] - width :], x[:width]
    xm = lax.ppermute(last, BOTH, route(1, False, spaces, filts))
    xp = lax.ppermute(first, BOTH, route(-1, False, spaces, filts))
    wide = jnp.concatenate([xm, x, xp], axis=0)
    off = lax.ppermute(lax.dynamic_slice_in_dim(wide, far, width, 1), BOTH, route(0, True, spaces, filts))
    pair = lax.ppermute(lax.dynamic_slice_in_dim(wide, near, width, 1), "filt", [(j, j ^ 1) for j in range(filts)])
    return x, xm, xp, off, pair


def steps(layer_input, first_kernel, second_kernel, cotangent):
    filts = lax.axis_size("filt")
    folded = layer_input.reshape(4, 4, 16, 256)
    pieces = surround(folded, 3)
    cot = cotangent.reshape(32, 2, 16, 32).transpose(2, 0, 1, 3).reshape(16, 16, 128)
    cot = lax.all_to_all(cot, "filt", 0, 0)
    cot = cot.reshape(512, 64)
    xc, slope, pooled = pl.pallas_call(
        first_kernel_body,
        out_shape=(
            jax.ShapeDtypeStruct((6, 6, 16, 512), BF16),
            jax.ShapeDtypeStruct((2, 4, 4, 16, 256), F32),
            jax.ShapeDtypeStruct((4, 4, 16, 256), BF16),
        ),
        in_specs=[VMEM] * 6,
        out_specs=(VMEM,) * 3,
        scratch_shapes=[pltpu.VMEM((10, 10, 16, 512), BF16)],
        compiler_params=pltpu.CompilerParams(vmem_limit_bytes=28 << 20),
        name="first_layer",
    )(*pieces, first_kernel)
    act, grad = pl.pallas_call(
        second_kernel_body,
        out_shape=(
            jax.ShapeDtypeStruct((512, 64), BF16),
            jax.ShapeDtypeStruct((2, 2, 16, 512), BF16),
        ),
        in_specs=[VMEM] * 2 + [HBM],
        out_specs=(VMEM,) * 2,
        scratch_shapes=[
            pltpu.VMEM((4, 4, 16, 768), BF16),
            pltpu.VMEM((512, 6912), BF16),
            pltpu.SemaphoreType.DMA((9,)),
        ],
        compiler_params=pltpu.CompilerParams(vmem_limit_bytes=28 << 20),
        name="second_layer",
    )(pooled, cot, second_kernel)
    grads = surround(grad, 1)
    keep, send = pl.pallas_call(
        backward_kernel,
        out_shape=(jax.ShapeDtypeStruct((128, 3456), BF16),) * 2,
        in_specs=[VMEM] * 7 + [HBM],
        out_specs=(VMEM,) * 2,
        scratch_shapes=[
            pltpu.VMEM((4, 4, 16, 1536), BF16),
            pltpu.VMEM((512, 6912), BF16),
            pltpu.SemaphoreType.DMA((9,)),
        ],
        compiler_params=pltpu.CompilerParams(vmem_limit_bytes=28 << 20),
        name="backward_layers",
    )(*grads, slope, xc, second_kernel)
    got = lax.ppermute(send, "filt", [(j, j ^ 1) for j in range(filts)])
    both = (keep.astype(F32) + got.astype(F32)).astype(BF16)
    spaces = lax.axis_size("space")
    groups = [[i * filts + j for i in range(spaces) for j in range(c, filts, 2)] for c in range(2)]
    parts = lax.all_to_all(both.reshape(64, 2, 3456), BOTH, 0, 0, axis_index_groups=groups)
    act = lax.all_to_all(act.reshape(16, 16, 128), "filt", 0, 0)
    activation = act.reshape(16, 32, 2, 32).transpose(1, 2, 0, 3).reshape(32, 2, 512).astype(F32)
    kernel_grad = parts.astype(F32).sum(axis=0)
    return (activation, kernel_grad)


def solution(mesh):
    return jax.shard_map(
        steps,
        mesh=mesh,
        in_specs=(P("space", "filt", None, None), P(), P(), P("filt", "space", None)),
        out_specs=(P("filt", "space", None), P(BOTH, None)),
        check_vma=False,
    )
```

profile of v0, /device:TPU:1, one launch (start us, length us, event | category | flops | bytes accessed | tf_op | source)
XLA Modules:
  0.0 112.0 jit_solution(14028515031917883665)
XLA Ops:
  0.6 1.0 fusion
  1.7 4.4 %collective-permute-start = (bf16[3,4,16,256]{3,2,1,0:T(8,128)(2,1)S(1)}, bf16[3,4,16,256]{3,2,1,0:T(8,128)(2,1)S(1)}, u32[]{:S(2)}, u32[]{:S(2)}) collective-permute-start(bf16[3,4,16,256]{3,2,1,0:T(8,128)(2,1)S(1)} %slice.19), channel_id=1, source_target_pairs={{0,16},{1,17},{2,18},{3,19},{4,20},{5,21},{6,22},{7,23},{8,24},{9,... | collective-permute-start | bytes 294920 | tf_op jit(solution)/shard_map/ppermute | solution.py:199
  6.1 1.4 %collective-permute-start.1 = (bf16[3,4,16,256]{3,2,1,0:T(8,128)(2,1)S(1)}, bf16[3,4,16,256]{3,2,1,0:T(8,128)(2,1)S(1)}, u32[]{:S(2)}, u32[]{:S(2)}) collective-permute-start(bf16[3,4,16,256]{3,2,1,0:T(8,128)(2,1)S(1)} %slice.21), channel_id=1, source_target_pairs={{16,0},{17,1},{18,2},{19,3},{20,4},{21,5},{22,6},{23,7},{24,8},{25... | collective-permute-start | bytes 294920 | tf_op jit(solution)/shard_map/ppermute | solution.py:200
  7.5 1.0 reshape.30.own
  8.6 3.0 %collective-permute-done.1.xp = bf16[3,4,16,256]{3,2,1,0:T(8,128)(2,1)S(1)} collective-permute-done((bf16[3,4,16,256]{3,2,1,0:T(8,128)(2,1)S(1)}, bf16[3,4,16,256]{3,2,1,0:T(8,128)(2,1)S(1)}, u32[]{:S(2)}, u32[]{:S(2)}) %collective-permute-start.1) | collective-permute-done | bytes 98336 | tf_op jit(solution)/shard_map/ppermute | solution.py:200
  11.6 0.8 constant_dynamic-slice_fusion.2
  12.5 2.1 %collective-permute-start.3 = (bf16[10,3,16,256]{3,2,1,0:T(8,128)(2,1)}, bf16[10,3,16,256]{3,2,1,0:T(8,128)(2,1)S(1)}, u32[]{:S(2)}, u32[]{:S(2)}) collective-permute-start(bf16[10,3,16,256]{3,2,1,0:T(8,128)(2,1)} %get-tuple-element.16), channel_id=1, source_target_pairs={{0,1},{1,0},{2,3},{3,2},{4,5},{5,4},{6,7},{7,6},{8,9},{9,8},{10,11... | collective-permute-start | bytes 737288 | tf_op jit(solution)/shard_map/ppermute | solution.py:203
  14.6 3.1 %collective-permute-start.2 = (bf16[10,3,16,256]{3,2,1,0:T(8,128)(2,1)}, bf16[10,3,16,256]{3,2,1,0:T(8,128)(2,1)S(1)}, u32[]{:S(2)}, u32[]{:S(2)}) collective-permute-start(bf16[10,3,16,256]{3,2,1,0:T(8,128)(2,1)} %get-tuple-element.17), channel_id=1, source_target_pairs={{1,2},{2,1},{3,4},{4,3},{5,6},{6,5},{7,8},{8,7},{9,10},{10,9},{11,... | collective-permute-start | bytes 737288 | tf_op jit(solution)/shard_map/ppermute | solution.py:202
  18.3 14.4 %all_to_all.15 = bf16[16,16,128]{2,1,0:T(8,128)(2,1)S(1)} all-to-all(bf16[16,16,128]{2,1,0:T(8,128)(2,1)S(1)} %reshape.32), channel_id=1, replica_groups=mesh['space'=8,'filt'=16] {'filt'}, dimensions={0} | all-to-all | bytes 131072 | tf_op jit(solution)/shard_map/all_to_all | solution.py:212
  32.9 0.7 copy-done.3
  33.5 0.7 copy-done.5
  34.2 0.9 copy-done.4
  35.2 0.9 copy-done.6
  36.1 4.8 %first_layer.1 = (bf16[6,6,16,512]{3,2,1,0:T(8,128)(2,1)S(1)}, f32[2,4,4,16,256]{4,3,2,1,0:T(8,128)S(1)}, bf16[4,4,16,256]{3,2,1,0:T(8,128)(2,1)S(1)}) custom-call(bf16[4,4,16,256]{3,2,1,0:T(8,128)(2,1)S(1)} %reshape.30.own, bf16[3,4,16,256]{3,2,1,0:T(8,128)(2,1)S(1)} %collective-permute-done.xm, bf16[3,4,16,256]{3,2,1,0:T(8,128)(2,1)S(1)} %collective-permute-done.1.xp, ...), custom_call_target="tpu_custom_call" | custom-call | tf_op jit(solution)/shard_map/first_layer/pallas_call | solution.py:214
  41.0 3.0 %copy-done = bf16[512,6912]{1,0:T(8,128)(2,1)S(1)} copy-done((bf16[512,6912]{1,0:T(8,128)(2,1)S(1)}, bf16[512,6912]{1,0:T(8,128)(2,1)}, u32[]{:S(2)}) %copy-start) | copy-done | bytes 7077912
  44.0 4.5 %second_layer.1 = (bf16[512,64]{1,0:T(8,128)(2,1)S(1)}, bf16[2,2,16,512]{3,2,1,0:T(8,128)(2,1)S(1)}) custom-call(bf16[4,4,16,256]{3,2,1,0:T(8,128)(2,1)S(1)} %get-tuple-element.9.pooled, bf16[512,64]{1,0:T(8,128)(2,1)S(1)} %reshape.33.cot, bf16[512,6912]{1,0:T(8,128)(2,1)S(1)} %copy-done), custom_call_target="tpu_custom_call" | custom-call | tf_op jit(solution)/shard_map/second_layer/pallas_call | solution.py:227
  48.6 3.3 %collective-permute-start.4 = (bf16[1,2,16,512]{3,2,1,0:T(8,128)(2,1)S(1)}, bf16[1,2,16,512]{3,2,1,0:T(8,128)(2,1)S(1)}, u32[]{:S(2)}, u32[]{:S(2)}) collective-permute-start(bf16[1,2,16,512]{3,2,1,0:T(8,128)(2,1)S(1)} %get-tuple-element.23), channel_id=1, source_target_pairs={{0,16},{1,17},{2,18},{3,19},{4,20},{5,21},{6,22},{7,23},{8,24},{9,... | collective-permute-start | bytes 98312 | tf_op jit(solution)/shard_map/ppermute | solution.py:199
  51.8 1.3 %collective-permute-start.5 = (bf16[1,2,16,512]{3,2,1,0:T(8,128)(2,1)S(1)}, bf16[1,2,16,512]{3,2,1,0:T(8,128)(2,1)S(1)}, u32[]{:S(2)}, u32[]{:S(2)}) collective-permute-start(bf16[1,2,16,512]{3,2,1,0:T(8,128)(2,1)S(1)} %get-tuple-element.22), channel_id=1, source_target_pairs={{16,0},{17,1},{18,2},{19,3},{20,4},{21,5},{22,6},{23,7},{24,8},{25... | collective-permute-start | bytes 98312 | tf_op jit(solution)/shard_map/ppermute | solution.py:200
  53.2 3.3 %collective-permute-done.5.xp = bf16[1,2,16,512]{3,2,1,0:T(8,128)(2,1)S(1)} collective-permute-done((bf16[1,2,16,512]{3,2,1,0:T(8,128)(2,1)S(1)}, bf16[1,2,16,512]{3,2,1,0:T(8,128)(2,1)S(1)}, u32[]{:S(2)}, u32[]{:S(2)}) %collective-permute-start.5) | collective-permute-done | bytes 32800 | tf_op jit(solution)/shard_map/ppermute | solution.py:200
  56.5 1.9 %collective-permute-start.7 = (bf16[4,1,16,512]{3,2,1,0:T(8,128)(2,1)S(1)}, bf16[4,1,16,512]{3,2,1,0:T(8,128)(2,1)S(1)}, u32[]{:S(2)}, u32[]{:S(2)}) collective-permute-start(bf16[4,1,16,512]{3,2,1,0:T(8,128)(2,1)S(1)} %get-tuple-element.18), channel_id=1, source_target_pairs={{0,1},{1,0},{2,3},{3,2},{4,5},{5,4},{6,7},{7,6},{8,9},{9,8},{10,11... | collective-permute-start | bytes 196616 | tf_op jit(solution)/shard_map/ppermute | solution.py:203
  58.4 2.1 %collective-permute-start.6 = (bf16[4,1,16,512]{3,2,1,0:T(8,128)(2,1)S(1)}, bf16[4,1,16,512]{3,2,1,0:T(8,128)(2,1)S(1)}, u32[]{:S(2)}, u32[]{:S(2)}) collective-permute-start(bf16[4,1,16,512]{3,2,1,0:T(8,128)(2,1)S(1)} %get-tuple-element.19), channel_id=1, source_target_pairs={{1,2},{2,1},{3,4},{4,3},{5,6},{6,5},{7,8},{8,7},{9,10},{10,9},{11,... | collective-permute-start | bytes 196616 | tf_op jit(solution)/shard_map/ppermute | solution.py:202
  60.5 3.5 %collective-permute-done.6.off = bf16[4,1,16,512]{3,2,1,0:T(8,128)(2,1)S(1)} collective-permute-done((bf16[4,1,16,512]{3,2,1,0:T(8,128)(2,1)S(1)}, bf16[4,1,16,512]{3,2,1,0:T(8,128)(2,1)S(1)}, u32[]{:S(2)}, u32[]{:S(2)}) %collective-permute-start.6) | collective-permute-done | bytes 65568 | tf_op jit(solution)/shard_map/ppermute | solution.py:202
  64.0 3.0 %copy-done.1 = bf16[512,6912]{1,0:T(8,128)(2,1)S(1)} copy-done((bf16[512,6912]{1,0:T(8,128)(2,1)S(1)}, bf16[512,6912]{1,0:T(8,128)(2,1)}, u32[]{:S(2)}) %copy-start.1) | copy-done | bytes 7077912
  67.0 6.4 %backward_layers.1 = (bf16[128,3456]{1,0:T(8,128)(2,1)S(1)}, bf16[128,3456]{1,0:T(8,128)(2,1)}) custom-call(bf16[2,2,16,512]{3,2,1,0:T(8,128)(2,1)S(1)} %get-tuple-element.11.own, bf16[1,2,16,512]{3,2,1,0:T(8,128)(2,1)S(1)} %collective-permute-done.4.xm, bf16[1,2,16,512]{3,2,1,0:T(8,128)(2,1)S(1)} %collective-permute-done.5.xp, ...), custom_call_target="tpu_custom_call" | custom-call | tf_op jit(solution)/shard_map/backward_layers/pallas_call | solution.py:244
  73.5 0.7 reshape.34
  74.2 6.6 %all-to-all-start.1 = ((bf16[16,16,128]{2,1,0:T(8,128)(2,1)}), bf16[16,16,128]{2,1,0:T(8,128)(2,1)S(1)}, u32[]{:S(2)}, u32[]{:S(2)}) async-start(bf16[16,16,128]{2,1,0:T(8,128)(2,1)} %reshape.34), calls=%async_computation.1 | async-start | bytes 131072 | tf_op jit(solution)/shard_map/all_to_all | solution.py:262
  81.1 1.3 %reshape.35 = bf16[64,2,3456]{2,1,0:T(2,128)(2,1)} reshape(bf16[128,3456]{1,0:T(8,128)(2,1)S(1)} %add_convert_fusion) | data formatting | bytes 1769472 | tf_op jit(solution)/shard_map/reshape | solution.py:261
  82.4 5.8 %all-to-all-done.1 = bf16[16,16,128]{2,1,0:T(8,128)(2,1)S(1)} async-done(((bf16[16,16,128]{2,1,0:T(8,128)(2,1)}), bf16[16,16,128]{2,1,0:T(8,128)(2,1)S(1)}, u32[]{:S(2)}, u32[]{:S(2)}) %all-to-all-start.1) | async-done | bytes 65568 | tf_op jit(solution)/shard_map/all_to_all | solution.py:262
  88.2 7.1 %all-to-all-start.2 = ((bf16[64,2,3456]{2,1,0:T(2,128)(2,1)}), bf16[64,2,3456]{2,1,0:T(2,128)(2,1)S(1)}, u32[]{:S(2)}, u32[]{:S(2)}) async-start(bf16[64,2,3456]{2,1,0:T(2,128)(2,1)} %reshape.35), calls=%async_computation.2 | async-start | bytes 1769472 | tf_op jit(solution)/shard_map/all_to_all | solution.py:261
  96.1 0.9 reshape.36
  97.0 13.7 %all-to-all-done.2 = bf16[64,2,3456]{2,1,0:T(2,128)(2,1)S(1)} async-done(((bf16[64,2,3456]{2,1,0:T(2,128)(2,1)}), bf16[64,2,3456]{2,1,0:T(2,128)(2,1)S(1)}, u32[]{:S(2)}, u32[]{:S(2)}) %all-to-all-start.2) | async-done | bytes 884768 | tf_op jit(solution)/shard_map/all_to_all | solution.py:261
  110.6 1.3 %convert_reduce_fusion = f32[2,3456]{1,0:T(2,128)} fusion(bf16[64,2,3456]{2,1,0:T(2,128)(2,1)S(1)} %all-to-all-done.2), kind=kLoop, calls=%fused_computation | loop fusion | flops 877824 | bytes 912384 | tf_op jit(solution)/shard_map/reduce_sum | solution.py:264
  (34 shorter events, 1.9 us)
Async XLA Ops:
  0.6 17.0 %copy-start.7 = (bf16[32,2,512]{2,1,0:T(2,128)(2,1)S(1)}, bf16[32,2,512]{2,1,0:T(2,128)(2,1)}, u32[]{:S(2)}) copy-start(bf16[32,2,512]{2,1,0:T(2,128)(2,1)} %param.7) | copy-start | bytes 196612
  1.7 6.8 %collective-permute-start = (bf16[3,4,16,256]{3,2,1,0:T(8,128)(2,1)S(1)}, bf16[3,4,16,256]{3,2,1,0:T(8,128)(2,1)S(1)}, u32[]{:S(2)}, u32[]{:S(2)}) collective-permute-start(bf16[3,4,16,256]{3,2,1,0:T(8,128)(2,1)S(1)} %slice.19), channel_id=1, source_target_pairs={{0,16},{1,17},{2,18},{3,19},{4,20},{5,21},{6,22},{7,23},{8,24},{9,... | collective-permute-start | bytes 294920 | tf_op jit(solution)/shard_map/ppermute | solution.py:199
  6.1 28.2 %copy-start.2 = (bf16[256,3456]{1,0:T(8,128)(2,1)S(1)}, bf16[256,3456]{1,0:T(8,128)(2,1)}, u32[]{:S(2)}) copy-start(bf16[256,3456]{1,0:T(8,128)(2,1)} %w1.1) | copy-start | bytes 5308420
  6.1 5.5 %collective-permute-start.1 = (bf16[3,4,16,256]{3,2,1,0:T(8,128)(2,1)S(1)}, bf16[3,4,16,256]{3,2,1,0:T(8,128)(2,1)S(1)}, u32[]{:S(2)}, u32[]{:S(2)}) collective-permute-start(bf16[3,4,16,256]{3,2,1,0:T(8,128)(2,1)S(1)} %slice.21), channel_id=1, source_target_pairs={{16,0},{17,1},{18,2},{19,3},{20,4},{21,5},{22,6},{23,7},{24,8},{25... | collective-permute-start | bytes 294920 | tf_op jit(solution)/shard_map/ppermute | solution.py:200
  12.5 20.4 %collective-permute-start.3 = (bf16[10,3,16,256]{3,2,1,0:T(8,128)(2,1)}, bf16[10,3,16,256]{3,2,1,0:T(8,128)(2,1)S(1)}, u32[]{:S(2)}, u32[]{:S(2)}) collective-permute-start(bf16[10,3,16,256]{3,2,1,0:T(8,128)(2,1)} %get-tuple-element.16), channel_id=1, source_target_pairs={{0,1},{1,0},{2,3},{3,2},{4,5},{5,4},{6,7},{7,6},{8,9},{9,8},{10,11... | collective-permute-start | bytes 737288 | tf_op jit(solution)/shard_map/ppermute | solution.py:203
  14.6 19.0 %collective-permute-start.2 = (bf16[10,3,16,256]{3,2,1,0:T(8,128)(2,1)}, bf16[10,3,16,256]{3,2,1,0:T(8,128)(2,1)S(1)}, u32[]{:S(2)}, u32[]{:S(2)}) collective-permute-start(bf16[10,3,16,256]{3,2,1,0:T(8,128)(2,1)} %get-tuple-element.17), channel_id=1, source_target_pairs={{1,2},{2,1},{3,4},{4,3},{5,6},{6,5},{7,8},{8,7},{9,10},{10,9},{11,... | collective-permute-start | bytes 737288 | tf_op jit(solution)/shard_map/ppermute | solution.py:202
  32.8 0.7 copy-start.3
  33.5 0.7 copy-start.5
  34.2 0.9 copy-start.4
  35.2 0.9 copy-start.6
  41.0 3.0 %copy-start = (bf16[512,6912]{1,0:T(8,128)(2,1)S(1)}, bf16[512,6912]{1,0:T(8,128)(2,1)}, u32[]{:S(2)}) copy-start(bf16[512,6912]{1,0:T(8,128)(2,1)} %w2_hbm.3) | copy-start | bytes 21233668
  48.6 4.6 %collective-permute-start.4 = (bf16[1,2,16,512]{3,2,1,0:T(8,128)(2,1)S(1)}, bf16[1,2,16,512]{3,2,1,0:T(8,128)(2,1)S(1)}, u32[]{:S(2)}, u32[]{:S(2)}) collective-permute-start(bf16[1,2,16,512]{3,2,1,0:T(8,128)(2,1)S(1)} %get-tuple-element.23), channel_id=1, source_target_pairs={{0,16},{1,17},{2,18},{3,19},{4,20},{5,21},{6,22},{7,23},{8,24},{9,... | collective-permute-start | bytes 98312 | tf_op jit(solution)/shard_map/ppermute | solution.py:199
  51.8 4.7 %collective-permute-start.5 = (bf16[1,2,16,512]{3,2,1,0:T(8,128)(2,1)S(1)}, bf16[1,2,16,512]{3,2,1,0:T(8,128)(2,1)S(1)}, u32[]{:S(2)}, u32[]{:S(2)}) collective-permute-start(bf16[1,2,16,512]{3,2,1,0:T(8,128)(2,1)S(1)} %get-tuple-element.22), channel_id=1, source_target_pairs={{16,0},{17,1},{18,2},{19,3},{20,4},{21,5},{22,6},{23,7},{24,8},{25... | collective-permute-start | bytes 98312 | tf_op jit(solution)/shard_map/ppermute | solution.py:200
  56.5 4.0 %collective-permute-start.7 = (bf16[4,1,16,512]{3,2,1,0:T(8,128)(2,1)S(1)}, bf16[4,1,16,512]{3,2,1,0:T(8,128)(2,1)S(1)}, u32[]{:S(2)}, u32[]{:S(2)}) collective-permute-start(bf16[4,1,16,512]{3,2,1,0:T(8,128)(2,1)S(1)} %get-tuple-element.18), channel_id=1, source_target_pairs={{0,1},{1,0},{2,3},{3,2},{4,5},{5,4},{6,7},{7,6},{8,9},{9,8},{10,11... | collective-permute-start | bytes 196616 | tf_op jit(solution)/shard_map/ppermute | solution.py:203
  58.4 5.6 %collective-permute-start.6 = (bf16[4,1,16,512]{3,2,1,0:T(8,128)(2,1)S(1)}, bf16[4,1,16,512]{3,2,1,0:T(8,128)(2,1)S(1)}, u32[]{:S(2)}, u32[]{:S(2)}) collective-permute-start(bf16[4,1,16,512]{3,2,1,0:T(8,128)(2,1)S(1)} %get-tuple-element.19), channel_id=1, source_target_pairs={{1,2},{2,1},{3,4},{4,3},{5,6},{6,5},{7,8},{8,7},{9,10},{10,9},{11,... | collective-permute-start | bytes 196616 | tf_op jit(solution)/shard_map/ppermute | solution.py:202
  64.0 3.0 %copy-start.1 = (bf16[512,6912]{1,0:T(8,128)(2,1)S(1)}, bf16[512,6912]{1,0:T(8,128)(2,1)}, u32[]{:S(2)}) copy-start(bf16[512,6912]{1,0:T(8,128)(2,1)} %w2_hbm.3) | copy-start | bytes 21233668
  73.4 7.5 %collective-permute-start.8 = (bf16[128,3456]{1,0:T(8,128)(2,1)}, bf16[128,3456]{1,0:T(8,128)(2,1)S(1)}, u32[]{:S(2)}, u32[]{:S(2)}) collective-permute-start(bf16[128,3456]{1,0:T(8,128)(2,1)} %get-tuple-element.15), channel_id=1, source_target_pairs={{0,1},{1,0},{2,3},{3,2},{4,5},{5,4},{6,7},{7,6},{8,9},{9,8},{10,11... | collective-permute-start | bytes 2654216 | tf_op jit(solution)/shard_map/ppermute | solution.py:257
  74.2 14.0 %all-to-all-start.1 = ((bf16[16,16,128]{2,1,0:T(8,128)(2,1)}), bf16[16,16,128]{2,1,0:T(8,128)(2,1)S(1)}, u32[]{:S(2)}, u32[]{:S(2)}) async-start(bf16[16,16,128]{2,1,0:T(8,128)(2,1)} %reshape.34), calls=%async_computation.1 | async-start | bytes 131072 | tf_op jit(solution)/shard_map/all_to_all | solution.py:262
  88.2 22.4 %all-to-all-start.2 = ((bf16[64,2,3456]{2,1,0:T(2,128)(2,1)}), bf16[64,2,3456]{2,1,0:T(2,128)(2,1)S(1)}, u32[]{:S(2)}, u32[]{:S(2)}) async-start(bf16[64,2,3456]{2,1,0:T(2,128)(2,1)} %reshape.35), calls=%async_computation.2 | async-start | bytes 1769472 | tf_op jit(solution)/shard_map/all_to_all | solution.py:261
where the time goes:
time: 113 us; the launch traced here: 112 us
  starting transfers between devices  33.3 us (29%)
  waiting for transfers between devices  29.4 us (26%)
  local copies, waits for them, and re-layouts  16.6 us (15%)
  Pallas kernels  15.7 us (14%)
  blocking collectives  14.4 us (13%)
  other arithmetic  1.53 us (1%)
    all_to_all x1, blocking collectives, steps(): cot = lax.all_to_all(cot, 'filt', 0, 0)  14.4 us
    all_to_all x1, waiting for transfers between devices, steps(): lax.all_to_all(both.reshape(64, 2, 3456), BOTH, 0, 0, axis_index_groups=g...  13.7 us
    unnamed x20, local copies, waits for them, and re-layouts  9.38 us
    ppermute x2, starting transfers between devices, surround(): xm = lax.ppermute(last, BOTH, route(1, False, spaces, filts))  7.62 us
    all_to_all x1, starting transfers between devices, steps(): lax.all_to_all(both.reshape(64, 2, 3456), BOTH, 0, 0, axis_index_groups=g...  7.09 us
    all_to_all x1, starting transfers between devices, steps(): act = lax.all_to_all(act.reshape(16, 16, 128), 'filt', 0, 0)  6.65 us
    ppermute x2, waiting for transfers between devices, surround(): xp = lax.ppermute(first, BOTH, route(-1, False, spaces, filts))  6.36 us
    pallas_call x1, Pallas kernels, steps(): pl.pallas_call(backward_kernel, out_shape=(jax.ShapeDtypeStruct((128, 345...  6.35 us
  transfers between devices with their start and end apart: 11, of which 5 were waited for; matrix products, arithmetic and copies ran while one was open for 5% of the time, Pallas kernels for 0%

commit v1 on v0

--- a/solution.py
+++ b/solution.py
@@ -189,7 +189,7 @@
     return pairs
 
 
-def surround(x, width):
+def surround(x, width, beside):
     spaces, filts = lax.axis_size("space"), lax.axis_size("filt")
     length = x.shape[1]
     parity = lax.rem(lax.axis_index("filt"), 2)
@@ -198,17 +198,18 @@
     last, first = x[x.shape[0] - width :], x[:width]
     xm = lax.ppermute(last, BOTH, route(1, False, spaces, filts))
     xp = lax.ppermute(first, BOTH, route(-1, False, spaces, filts))
+    xp, beside = lax.optimization_barrier((xp, beside))
     wide = jnp.concatenate([xm, x, xp], axis=0)
     off = lax.ppermute(lax.dynamic_slice_in_dim(wide, far, width, 1), BOTH, route(0, True, spaces, filts))
     pair = lax.ppermute(lax.dynamic_slice_in_dim(wide, near, width, 1), "filt", [(j, j ^ 1) for j in range(filts)])
-    return x, xm, xp, off, pair
+    return (x, xm, xp, off, pair), beside
 
 
 def steps(layer_input, first_kernel, second_kernel, cotangent):
     filts = lax.axis_size("filt")
     folded = layer_input.reshape(4, 4, 16, 256)
-    pieces = surround(folded, 3)
     cot = cotangent.reshape(32, 2, 16, 32).transpose(2, 0, 1, 3).reshape(16, 16, 128)
+    pieces, cot = surround(folded, 3, cot)
     cot = lax.all_to_all(cot, "filt", 0, 0)
     cot = cot.reshape(512, 64)
     xc, slope, pooled = pl.pallas_call(
@@ -221,7 +222,7 @@
         in_specs=[VMEM] * 6,
         out_specs=(VMEM,) * 3,
         scratch_shapes=[pltpu.VMEM((10, 10, 16, 512), BF16)],
-        compiler_params=pltpu.CompilerParams(vmem_limit_bytes=28 << 20),
+        compiler_params=pltpu.CompilerParams(vmem_limit_bytes=40 << 20),
         name="first_layer",
     )(*pieces, first_kernel)
     act, grad = pl.pallas_call(
@@ -237,10 +238,10 @@
             pltpu.VMEM((512, 6912), BF16),
             pltpu.SemaphoreType.DMA((9,)),
         ],
-        compiler_params=pltpu.CompilerParams(vmem_limit_bytes=28 << 20),
+        compiler_params=pltpu.CompilerParams(vmem_limit_bytes=48 << 20),
         name="second_layer",
     )(pooled, cot, second_kernel)
-    grads = surround(grad, 1)
+    grads, act = surround(grad, 1, act.reshape(16, 16, 128))
     keep, send = pl.pallas_call(
         backward_kernel,
         out_shape=(jax.ShapeDtypeStruct((128, 3456), BF16),) * 2,
@@ -251,7 +252,7 @@
             pltpu.VMEM((512, 6912), BF16),
             pltpu.SemaphoreType.DMA((9,)),
         ],
-        compiler_params=pltpu.CompilerParams(vmem_limit_bytes=28 << 20),
+        compiler_params=pltpu.CompilerParams(vmem_limit_bytes=48 << 20),
         name="backward_layers",
     )(*grads, slope, xc, second_kernel)
     got = lax.ppermute(send, "filt", [(j, j ^ 1) for j in range(filts)])
@@ -259,7 +260,7 @@
     spaces = lax.axis_size("space")
     groups = [[i * filts + j for i in range(spaces) for j in range(c, filts, 2)] for c in range(2)]
     parts = lax.all_to_all(both.reshape(64, 2, 3456), BOTH, 0, 0, axis_index_groups=groups)
-    act = lax.all_to_all(act.reshape(16, 16, 128), "filt", 0, 0)
+    act = lax.all_to_all(act, "filt", 0, 0)
     activation = act.reshape(16, 32, 2, 32).transpose(1, 2, 0, 3).reshape(32, 2, 512).astype(F32)
     kernel_grad = parts.astype(F32).sum(axis=0)
     return (activation, kernel_grad)

time: 113 us -> 106 us (0.938)
  local copies, waits for them, and re-layouts: 16.6 us -> 11.4 us
  waiting for transfers between devices: 29.4 us -> 24.2 us
  starting transfers between devices: 33.3 us -> 35.9 us
    ppermute x2, waiting for transfers between devices: 6.36 us -> 0.01 us  [surround(): xp = lax.ppermute(first, BOTH, route(-1, False, spaces, filts))]
    unnamed x20 -> x14, local copies, waits for them, and re-layouts: 9.38 us -> 3.29 us
    all_to_all x1, starting transfers between devices: 7.09 us -> 10.1 us  [steps(): lax.all_to_all(both.reshape(64, 2, 3456), BOTH, 0, 0, axis_index_groups=g...]
    ppermute x2, starting transfers between devices: 4 us -> 1.96 us  [surround(): lax.ppermute(lax.dynamic_slice_in_dim(wide, near, width, 1), 'filt', [(j,...]
    ppermute x2, starting transfers between devices: 7.62 us -> 9.27 us  [surround(): xm = lax.ppermute(last, BOTH, route(1, False, spaces, filts))]
    ppermute x2, waiting for transfers between devices: 0.01 us -> 1.2 us  [surround(): xm = lax.ppermute(last, BOTH, route(1, False, spaces, filts))]
  transfers between devices with their start and end apart: 11 -> 11, of which waited for: 5 -> 5; matrix products, arithmetic and copies ran while one was open for 5% -> 6% of each run, Pallas kernels for 0% -> 0%
where the time goes in v1:
time: 106 us; the launch traced here: 105 us
  starting transfers between devices  35.9 us (34%)
  waiting for transfers between devices  24.2 us (23%)
  Pallas kernels  16.2 us (15%)
  blocking collectives  14.4 us (14%)
  local copies, waits for them, and re-layouts  11.4 us (11%)
  other arithmetic  1.53 us (1%)
    all_to_all x1, blocking collectives, steps(): cot = lax.all_to_all(cot, 'filt', 0, 0)  14.4 us
    all_to_all x1, waiting for transfers between devices, steps(): lax.all_to_all(both.reshape(64, 2, 3456), BOTH, 0, 0, axis_index_groups=g...  13.7 us
    all_to_all x1, starting transfers between devices, steps(): lax.all_to_all(both.reshape(64, 2, 3456), BOTH, 0, 0, axis_index_groups=g...  10.1 us
    ppermute x2, starting transfers between devices, surround(): xm = lax.ppermute(last, BOTH, route(1, False, spaces, filts))  9.27 us
    all_to_all x1, starting transfers between devices, steps(): act = lax.all_to_all(act, 'filt', 0, 0)  6.66 us
    pallas_call x1, Pallas kernels, steps(): pl.pallas_call(backward_kernel, out_shape=(jax.ShapeDtypeStruct((128, 345...  6 us
    all_to_all x1, waiting for transfers between devices, steps(): act = lax.all_to_all(act, 'filt', 0, 0)  5.85 us
    pallas_call x1, Pallas kernels, steps(): pl.pallas_call(second_kernel_body, out_shape=(jax.ShapeDtypeStruct((512,...  5.32 us
  transfers between devices with their start and end apart: 11, of which 5 were waited for; matrix products, arithmetic and copies ran while one was open for 6% of the time, Pallas kernels for 0%

profile of v1, /device:TPU:1, one launch (start us, length us, event | category | flops | bytes accessed | tf_op | source)
XLA Modules:
  0.0 104.6 jit_solution(8286649276356371887)
XLA Ops:
  0.6 1.0 fusion
  1.7 1.3 %collective-permute-start.1 = (bf16[3,4,16,256]{3,2,1,0:T(8,128)(2,1)S(1)}, bf16[3,4,16,256]{3,2,1,0:T(8,128)(2,1)S(1)}, u32[]{:S(2)}, u32[]{:S(2)}) collective-permute-start(bf16[3,4,16,256]{3,2,1,0:T(8,128)(2,1)S(1)} %slice.21), channel_id=1, source_target_pairs={{16,0},{17,1},{18,2},{19,3},{20,4},{21,5},{22,6},{23,7},{24,8},{25... | collective-permute-start | bytes 294920 | tf_op jit(solution)/shard_map/ppermute | solution.py:200
  3.0 5.1 %collective-permute-start = (bf16[3,4,16,256]{3,2,1,0:T(8,128)(2,1)S(1)}, bf16[3,4,16,256]{3,2,1,0:T(8,128)(2,1)S(1)}, u32[]{:S(2)}, u32[]{:S(2)}) collective-permute-start(bf16[3,4,16,256]{3,2,1,0:T(8,128)(2,1)S(1)} %slice.19), channel_id=1, source_target_pairs={{0,16},{1,17},{2,18},{3,19},{4,20},{5,21},{6,22},{7,23},{8,24},{9,... | collective-permute-start | bytes 294920 | tf_op jit(solution)/shard_map/ppermute | solution.py:199
  8.2 1.0 reshape.30.own
  9.1 1.1 %reshape.31 = bf16[32,2,16,32]{3,2,1,0:T(8,128)(2,1)S(1)} reshape(bf16[32,2,512]{2,1,0:T(2,128)(2,1)} %param.7) | data formatting | bytes 131072 | tf_op jit(solution)/shard_map/reshape | solution.py:211
  10.6 0.9 collective-permute-done.xm
  11.6 0.9 constant_dynamic-slice_fusion.2
  12.4 0.6 collective-permute-start.3
  13.0 3.1 %collective-permute-start.2 = (bf16[10,3,16,256]{3,2,1,0:T(8,128)(2,1)}, bf16[10,3,16,256]{3,2,1,0:T(8,128)(2,1)S(1)}, u32[]{:S(2)}, u32[]{:S(2)}) collective-permute-start(bf16[10,3,16,256]{3,2,1,0:T(8,128)(2,1)} %get-tuple-element.25), channel_id=1, source_target_pairs={{1,2},{2,1},{3,4},{4,3},{5,6},{6,5},{7,8},{8,7},{9,10},{10,9},{11,... | collective-permute-start | bytes 737288 | tf_op jit(solution)/shard_map/ppermute | solution.py:203
  16.1 14.4 %all_to_all.15 = bf16[16,16,128]{2,1,0:T(8,128)(2,1)S(1)} all-to-all(bf16[16,16,128]{2,1,0:T(8,128)(2,1)S(1)} %reshape.32), channel_id=1, replica_groups=mesh['space'=8,'filt'=16] {'filt'}, dimensions={0} | all-to-all | bytes 131072 | tf_op jit(solution)/shard_map/all_to_all | solution.py:213
  30.7 0.7 copy-done.1
  31.3 0.7 copy-done.3
  32.0 0.9 copy-done.2
  33.0 0.9 copy-done.4
  33.9 4.8 %first_layer.1 = (bf16[6,6,16,512]{3,2,1,0:T(8,128)(2,1)S(1)}, f32[2,4,4,16,256]{4,3,2,1,0:T(8,128)S(1)}, bf16[4,4,16,256]{3,2,1,0:T(8,128)(2,1)S(1)}) custom-call(bf16[4,4,16,256]{3,2,1,0:T(8,128)(2,1)S(1)} %reshape.30.own, bf16[3,4,16,256]{3,2,1,0:T(8,128)(2,1)S(1)} %collective-permute-done.xm, bf16[3,4,16,256]{3,2,1,0:T(8,128)(2,1)S(1)} %collective-permute-done.1.xp, ...), custom_call_target="tpu_custom_call" | custom-call | tf_op jit(solution)/shard_map/first_layer/pallas_call | solution.py:215
  38.8 5.3 %second_layer.1 = (bf16[512,64]{1,0:T(8,128)(2,1)S(1)}, bf16[2,2,16,512]{3,2,1,0:T(8,128)(2,1)S(1)}) custom-call(bf16[4,4,16,256]{3,2,1,0:T(8,128)(2,1)S(1)} %get-tuple-element.14.pooled, bf16[512,64]{1,0:T(8,128)(2,1)S(1)} %reshape.33.cot, bf16[512,6912]{1,0:T(8,128)(2,1)} %w2_hbm.3), custom_call_target="tpu_custom_call" | custom-call | tf_op jit(solution)/shard_map/second_layer/pallas_call | solution.py:228
  44.1 1.3 %collective-permute-start.4 = (bf16[1,2,16,512]{3,2,1,0:T(8,128)(2,1)S(1)}, bf16[1,2,16,512]{3,2,1,0:T(8,128)(2,1)S(1)}, u32[]{:S(2)}, u32[]{:S(2)}) collective-permute-start(bf16[1,2,16,512]{3,2,1,0:T(8,128)(2,1)S(1)} %get-tuple-element.31), channel_id=1, source_target_pairs={{16,0},{17,1},{18,2},{19,3},{20,4},{21,5},{22,6},{23,7},{24,8},{25... | collective-permute-start | bytes 98312 | tf_op jit(solution)/shard_map/ppermute | solution.py:200
  45.4 4.1 %collective-permute-start.5 = (bf16[1,2,16,512]{3,2,1,0:T(8,128)(2,1)S(1)}, bf16[1,2,16,512]{3,2,1,0:T(8,128)(2,1)S(1)}, u32[]{:S(2)}, u32[]{:S(2)}) collective-permute-start(bf16[1,2,16,512]{3,2,1,0:T(8,128)(2,1)S(1)} %get-tuple-element.30), channel_id=1, source_target_pairs={{0,16},{1,17},{2,18},{3,19},{4,20},{5,21},{6,22},{7,23},{8,24},{9,... | collective-permute-start | bytes 98312 | tf_op jit(solution)/shard_map/ppermute | solution.py:199
  49.6 0.7 reshape.34
  50.7 1.4 %collective-permute-start.7 = (bf16[4,1,16,512]{3,2,1,0:T(8,128)(2,1)S(1)}, bf16[4,1,16,512]{3,2,1,0:T(8,128)(2,1)S(1)}, u32[]{:S(2)}, u32[]{:S(2)}) collective-permute-start(bf16[4,1,16,512]{3,2,1,0:T(8,128)(2,1)S(1)} %get-tuple-element.26), channel_id=1, source_target_pairs={{0,1},{1,0},{2,3},{3,2},{4,5},{5,4},{6,7},{7,6},{8,9},{9,8},{10,11... | collective-permute-start | bytes 196616 | tf_op jit(solution)/shard_map/ppermute | solution.py:204
  52.1 2.1 %collective-permute-start.6 = (bf16[4,1,16,512]{3,2,1,0:T(8,128)(2,1)S(1)}, bf16[4,1,16,512]{3,2,1,0:T(8,128)(2,1)S(1)}, u32[]{:S(2)}, u32[]{:S(2)}) collective-permute-start(bf16[4,1,16,512]{3,2,1,0:T(8,128)(2,1)S(1)} %get-tuple-element.27), channel_id=1, source_target_pairs={{1,2},{2,1},{3,4},{4,3},{5,6},{6,5},{7,8},{8,7},{9,10},{10,9},{11,... | collective-permute-start | bytes 196616 | tf_op jit(solution)/shard_map/ppermute | solution.py:203
  54.2 3.5 %collective-permute-done.6.off = bf16[4,1,16,512]{3,2,1,0:T(8,128)(2,1)S(1)} collective-permute-done((bf16[4,1,16,512]{3,2,1,0:T(8,128)(2,1)S(1)}, bf16[4,1,16,512]{3,2,1,0:T(8,128)(2,1)S(1)}, u32[]{:S(2)}, u32[]{:S(2)}) %collective-permute-start.6) | collective-permute-done | bytes 65568 | tf_op jit(solution)/shard_map/ppermute | solution.py:203
  57.6 6.0 %backward_layers.1 = (bf16[128,3456]{1,0:T(8,128)(2,1)S(1)}, bf16[128,3456]{1,0:T(8,128)(2,1)S(1)}) custom-call(bf16[2,2,16,512]{3,2,1,0:T(8,128)(2,1)S(1)} %get-tuple-element.16.own, bf16[1,2,16,512]{3,2,1,0:T(8,128)(2,1)S(1)} %collective-permute-done.5.xm, bf16[1,2,16,512]{3,2,1,0:T(8,128)(2,1)S(1)} %collective-permute-done.4.xp, ...), custom_call_target="tpu_custom_call" | custom-call | tf_op jit(solution)/shard_map/backward_layers/pallas_call | solution.py:245
  63.7 6.7 %all-to-all-start.1 = ((bf16[16,16,128]{2,1,0:T(8,128)(2,1)}), bf16[16,16,128]{2,1,0:T(8,128)(2,1)S(1)}, u32[]{:S(2)}, u32[]{:S(2)}) async-start(bf16[16,16,128]{2,1,0:T(8,128)(2,1)} %reshape.34), calls=%async_computation.1 | async-start | bytes 131072 | tf_op jit(solution)/shard_map/all_to_all | solution.py:263
  70.6 1.3 %reshape.35 = bf16[64,2,3456]{2,1,0:T(2,128)(2,1)} reshape(bf16[128,3456]{1,0:T(8,128)(2,1)S(1)} %add_convert_fusion) | data formatting | bytes 1769472 | tf_op jit(solution)/shard_map/reshape | solution.py:262
  71.9 5.9 %all-to-all-done.1 = bf16[16,16,128]{2,1,0:T(8,128)(2,1)S(1)} async-done(((bf16[16,16,128]{2,1,0:T(8,128)(2,1)}), bf16[16,16,128]{2,1,0:T(8,128)(2,1)S(1)}, u32[]{:S(2)}, u32[]{:S(2)}) %all-to-all-start.1) | async-done | bytes 65568 | tf_op jit(solution)/shard_map/all_to_all | solution.py:263
  77.7 10.1 %all-to-all-start.2 = ((bf16[64,2,3456]{2,1,0:T(2,128)(2,1)}), bf16[64,2,3456]{2,1,0:T(2,128)(2,1)S(1)}, u32[]{:S(2)}, u32[]{:S(2)}) async-start(bf16[64,2,3456]{2,1,0:T(2,128)(2,1)} %reshape.35), calls=%async_computation.2 | async-start | bytes 1769472 | tf_op jit(solution)/shard_map/all_to_all | solution.py:262
  87.9 0.4 reshape.37
  88.3 0.3 copy.9
  88.6 0.9 reshape.36
  89.6 13.7 %all-to-all-done.2 = bf16[64,2,3456]{2,1,0:T(2,128)(2,1)S(1)} async-done(((bf16[64,2,3456]{2,1,0:T(2,128)(2,1)}), bf16[64,2,3456]{2,1,0:T(2,128)(2,1)S(1)}, u32[]{:S(2)}, u32[]{:S(2)}) %all-to-all-start.2) | async-done | bytes 884768 | tf_op jit(solution)/shard_map/all_to_all | solution.py:262
  103.2 1.3 %convert_reduce_fusion = f32[2,3456]{1,0:T(2,128)} fusion(bf16[64,2,3456]{2,1,0:T(2,128)(2,1)S(1)} %all-to-all-done.2), kind=kLoop, calls=%fused_computation | loop fusion | flops 877824 | bytes 912384 | tf_op jit(solution)/shard_map/reduce_sum | solution.py:265
  (28 shorter events, 1.3 us)
Async XLA Ops:
  1.7 9.0 %collective-permute-start.1 = (bf16[3,4,16,256]{3,2,1,0:T(8,128)(2,1)S(1)}, bf16[3,4,16,256]{3,2,1,0:T(8,128)(2,1)S(1)}, u32[]{:S(2)}, u32[]{:S(2)}) collective-permute-start(bf16[3,4,16,256]{3,2,1,0:T(8,128)(2,1)S(1)} %slice.21), channel_id=1, source_target_pairs={{16,0},{17,1},{18,2},{19,3},{20,4},{21,5},{22,6},{23,7},{24,8},{25... | collective-permute-start | bytes 294920 | tf_op jit(solution)/shard_map/ppermute | solution.py:200
  3.0 29.0 %copy-start = (bf16[256,3456]{1,0:T(8,128)(2,1)S(1)}, bf16[256,3456]{1,0:T(8,128)(2,1)}, u32[]{:S(2)}) copy-start(bf16[256,3456]{1,0:T(8,128)(2,1)} %w1.1) | copy-start | bytes 5308420
  3.0 8.5 %collective-permute-start = (bf16[3,4,16,256]{3,2,1,0:T(8,128)(2,1)S(1)}, bf16[3,4,16,256]{3,2,1,0:T(8,128)(2,1)S(1)}, u32[]{:S(2)}, u32[]{:S(2)}) collective-permute-start(bf16[3,4,16,256]{3,2,1,0:T(8,128)(2,1)S(1)} %slice.19), channel_id=1, source_target_pairs={{0,16},{1,17},{2,18},{3,19},{4,20},{5,21},{6,22},{7,23},{8,24},{9,... | collective-permute-start | bytes 294920 | tf_op jit(solution)/shard_map/ppermute | solution.py:199
  12.4 18.2 %collective-permute-start.3 = (bf16[10,3,16,256]{3,2,1,0:T(8,128)(2,1)}, bf16[10,3,16,256]{3,2,1,0:T(8,128)(2,1)S(1)}, u32[]{:S(2)}, u32[]{:S(2)}) collective-permute-start(bf16[10,3,16,256]{3,2,1,0:T(8,128)(2,1)} %get-tuple-element.24), channel_id=1, source_target_pairs={{0,1},{1,0},{2,3},{3,2},{4,5},{5,4},{6,7},{7,6},{8,9},{9,8},{10,11... | collective-permute-start | bytes 737288 | tf_op jit(solution)/shard_map/ppermute | solution.py:204
  13.0 18.3 %collective-permute-start.2 = (bf16[10,3,16,256]{3,2,1,0:T(8,128)(2,1)}, bf16[10,3,16,256]{3,2,1,0:T(8,128)(2,1)S(1)}, u32[]{:S(2)}, u32[]{:S(2)}) collective-permute-start(bf16[10,3,16,256]{3,2,1,0:T(8,128)(2,1)} %get-tuple-element.25), channel_id=1, source_target_pairs={{1,2},{2,1},{3,4},{4,3},{5,6},{6,5},{7,8},{8,7},{9,10},{10,9},{11,... | collective-permute-start | bytes 737288 | tf_op jit(solution)/shard_map/ppermute | solution.py:203
  30.6 0.7 copy-start.1
  31.3 0.7 copy-start.3
  32.0 0.9 copy-start.2
  33.0 0.9 copy-start.4
  44.1 6.2 %collective-permute-start.4 = (bf16[1,2,16,512]{3,2,1,0:T(8,128)(2,1)S(1)}, bf16[1,2,16,512]{3,2,1,0:T(8,128)(2,1)S(1)}, u32[]{:S(2)}, u32[]{:S(2)}) collective-permute-start(bf16[1,2,16,512]{3,2,1,0:T(8,128)(2,1)S(1)} %get-tuple-element.31), channel_id=1, source_target_pairs={{16,0},{17,1},{18,2},{19,3},{20,4},{21,5},{22,6},{23,7},{24,8},{25... | collective-permute-start | bytes 98312 | tf_op jit(solution)/shard_map/ppermute | solution.py:200
  45.4 5.2 %collective-permute-start.5 = (bf16[1,2,16,512]{3,2,1,0:T(8,128)(2,1)S(1)}, bf16[1,2,16,512]{3,2,1,0:T(8,128)(2,1)S(1)}, u32[]{:S(2)}, u32[]{:S(2)}) collective-permute-start(bf16[1,2,16,512]{3,2,1,0:T(8,128)(2,1)S(1)} %get-tuple-element.30), channel_id=1, source_target_pairs={{0,16},{1,17},{2,18},{3,19},{4,20},{5,21},{6,22},{7,23},{8,24},{9,... | collective-permute-start | bytes 98312 | tf_op jit(solution)/shard_map/ppermute | solution.py:199
  50.7 3.5 %collective-permute-start.7 = (bf16[4,1,16,512]{3,2,1,0:T(8,128)(2,1)S(1)}, bf16[4,1,16,512]{3,2,1,0:T(8,128)(2,1)S(1)}, u32[]{:S(2)}, u32[]{:S(2)}) collective-permute-start(bf16[4,1,16,512]{3,2,1,0:T(8,128)(2,1)S(1)} %get-tuple-element.26), channel_id=1, source_target_pairs={{0,1},{1,0},{2,3},{3,2},{4,5},{5,4},{6,7},{7,6},{8,9},{9,8},{10,11... | collective-permute-start | bytes 196616 | tf_op jit(solution)/shard_map/ppermute | solution.py:204
  52.1 5.6 %collective-permute-start.6 = (bf16[4,1,16,512]{3,2,1,0:T(8,128)(2,1)S(1)}, bf16[4,1,16,512]{3,2,1,0:T(8,128)(2,1)S(1)}, u32[]{:S(2)}, u32[]{:S(2)}) collective-permute-start(bf16[4,1,16,512]{3,2,1,0:T(8,128)(2,1)S(1)} %get-tuple-element.27), channel_id=1, source_target_pairs={{1,2},{2,1},{3,4},{4,3},{5,6},{6,5},{7,8},{8,7},{9,10},{10,9},{11,... | collective-permute-start | bytes 196616 | tf_op jit(solution)/shard_map/ppermute | solution.py:203
  63.6 6.8 %collective-permute-start.8 = (bf16[128,3456]{1,0:T(8,128)(2,1)S(1)}, bf16[128,3456]{1,0:T(8,128)(2,1)S(1)}, u32[]{:S(2)}, u32[]{:S(2)}) collective-permute-start(bf16[128,3456]{1,0:T(8,128)(2,1)S(1)} %get-tuple-element.23), channel_id=1, source_target_pairs={{0,1},{1,0},{2,3},{3,2},{4,5},{5,4},{6,7},{7,6},{8,9},{9,8},{10,11... | collective-permute-start | bytes 2654216 | tf_op jit(solution)/shard_map/ppermute | solution.py:258
  63.7 14.0 %all-to-all-start.1 = ((bf16[16,16,128]{2,1,0:T(8,128)(2,1)}), bf16[16,16,128]{2,1,0:T(8,128)(2,1)S(1)}, u32[]{:S(2)}, u32[]{:S(2)}) async-start(bf16[16,16,128]{2,1,0:T(8,128)(2,1)} %reshape.34), calls=%async_computation.1 | async-start | bytes 131072 | tf_op jit(solution)/shard_map/all_to_all | solution.py:263
  77.7 25.5 %all-to-all-start.2 = ((bf16[64,2,3456]{2,1,0:T(2,128)(2,1)}), bf16[64,2,3456]{2,1,0:T(2,128)(2,1)S(1)}, u32[]{:S(2)}, u32[]{:S(2)}) async-start(bf16[64,2,3456]{2,1,0:T(2,128)(2,1)} %reshape.35), calls=%async_computation.2 | async-start | bytes 1769472 | tf_op jit(solution)/shard_map/all_to_all | solution.py:262
